TPU v7x, 256 devices: a whole 4x4x8 slice. The times are simulated.
256 devices in a mesh: pair: 32 (over z, y), red: 8 (over x, core).
Axes of the slice: x: 4, y: 4, z: 8, core: 2. Of those that a mesh axis runs over, the one named last changes fastest.
Arguments:
- amplitudes: bfloat16 [2048, 512, 640], P('pair', 'red'), may hold values from -6 to 6
- cycle_integrals: bfloat16 [640, 640], P('pair'), may hold values from -0.5 to 0.5
- ladder_integrals: bfloat16 [32, 8, 1280, 512], P('pair', 'red'), may hold values from -0.125 to 0.125
- orbital_irrep: int32 [640], replicated, may hold values from 0 to 7, as said below
- pair_irrep: int32 [2048], P('pair'), may hold values from 0 to 7, as said below
- tile_owners: int32 [8, 320], replicated, may hold values from 0 to 319, each once within a row
- ladder_tiles: int32 [32, 4], replicated, may hold values from 0 to 2559
Outputs:
- ladder_block: bfloat16 [32, 2048, 512], P('pair', 'red')
Inputs may be any that keep to these rules, and one draw needn't show every extreme that they name: Each row of tile_owners is a permutation of 0 .. 319. `orbital_irrep`: nondecreasing along the virtual orbitals; the first is 0 and the last 7. A program must be right for any labels meeting these rules, including one irrep holding nearly all orbitals. `pair_irrep`: A program must be right for any labels in the range, in any mixture.
All inputs are finite; a program needn't handle non-finite values.
Results may differ from a plain program's by a relative error of at most 0.019.
Values may be sent and summed in bfloat16 or wider, within the bound.
A program may use at most 128 MiB of HBM per device.

v0:
```python
import jax
import jax.numpy as jnp
from jax import lax
from jax.sharding import PartitionSpec as P


def irrep_lookup(irreps, indices):
    table_ids = jnp.arange(irreps.shape[0], dtype=jnp.int32)
    return jnp.sum(jnp.where(indices[..., None] == table_ids, irreps, 0), axis=-1)


def shards(
    amplitudes,
    cycle_integrals,
    ladder_integrals,
    orbital_irrep,
    pair_irrep,
    tile_owners,
    ladder_tiles,
):
    pair_count = lax.axis_size("pair")
    pair_index = lax.axis_index("pair")
    red_index = lax.axis_index("red")
    local_pairs, slab_rows, width_all = amplitudes.shape
    block_count = width_all // 128
    a_local = red_index * slab_rows + jnp.arange(slab_rows, dtype=jnp.int32)
    irrep_slab = irrep_lookup(orbital_irrep, a_local)
    allowed = (
        jnp.bitwise_xor(irrep_slab[:, None], orbital_irrep[None, :])[None]
        == pair_irrep[:, None, None]
    )
    symmetric = jnp.where(allowed, amplitudes, jnp.zeros_like(amplitudes))
    cycle_rows = cycle_integrals.shape[0]
    c_local = pair_index * cycle_rows + jnp.arange(cycle_rows, dtype=jnp.int32)
    cycle_keep = irrep_lookup(orbital_irrep, c_local)[:, None] == orbital_irrep[None, :]
    blocked = jnp.where(cycle_keep, cycle_integrals, jnp.zeros_like(cycle_integrals))
    flattened = symmetric.reshape(local_pairs * slab_rows, width_all)
    gathered_cycle = lax.all_gather(blocked, "pair", axis=0, tiled=True)
    cycle = jnp.dot(flattened, gathered_cycle, preferred_element_type=jnp.float32)
    dressed = (flattened.astype(jnp.float32) + cycle).astype(jnp.bfloat16)
    tiles_local = dressed.reshape(local_pairs, slab_rows * block_count, 128)
    slot_order = lax.dynamic_index_in_dim(tile_owners, red_index, 0, keepdims=False)
    owned_count = slot_order.shape[0] // pair_count
    ordered = jnp.take(tiles_local, slot_order, axis=1).reshape(
        local_pairs, pair_count, owned_count, 128
    )
    lane_ids = jnp.arange(128, dtype=jnp.int32)
    mine_tiles = lax.dynamic_slice_in_dim(slot_order, pair_index * owned_count, owned_count, 0)
    a_rows = red_index * slab_rows + mine_tiles // block_count
    b_cols = (mine_tiles % block_count)[:, None] * 128 + lane_ids
    irrep_cd = jnp.bitwise_xor(
        irrep_lookup(orbital_irrep, a_rows)[:, None], irrep_lookup(orbital_irrep, b_cols)
    ).reshape(-1)
    batch_ids = ladder_tiles[pair_index]
    a_out = batch_ids // block_count
    b_out = (batch_ids % block_count)[:, None] * 128 + lane_ids
    irrep_ab = jnp.bitwise_xor(
        irrep_lookup(orbital_irrep, a_out)[:, None], irrep_lookup(orbital_irrep, b_out)
    ).reshape(-1)
    weights = ladder_integrals[0, 0]
    masked = jnp.where(irrep_cd[:, None] == irrep_ab[None, :], weights, jnp.zeros_like(weights))
    total_rows = local_pairs * pair_count
    received = lax.all_to_all(ordered, "pair", split_axis=1, concat_axis=0, tiled=True)
    owned = received.reshape(total_rows, owned_count * 128)
    result = lax.psum_scatter(
        jnp.dot(owned, masked, preferred_element_type=jnp.float32).astype(jnp.bfloat16),
        "red",
        scatter_dimension=0,
        tiled=True,
    )
    return result[None]


def solution(mesh):
    return jax.shard_map(
        shards,
        mesh=mesh,
        in_specs=(
            P("pair", "red", None),
            P("pair", None),
            P("pair", "red", None, None),
            P(),
            P("pair"),
            P(),
            P(),
        ),
        out_specs=P("pair", "red", None),
        check_vma=False,
    )
```

profile of v0, /device:TPU:8, one launch (start us, length us, event | category | flops | bytes accessed | tf_op | source)
XLA Modules:
  0.0 275.5 jit_solution(3836330692513094179)
XLA Ops:
  6.5 0.7 fusion.14
  7.3 0.7 dynamic-slice_reduce_fusion
  8.0 0.9 select_reduce_fusion.2
  8.9 0.8 broadcast_xor_fusion
  9.7 0.9 select_reduce_fusion.3
  10.5 0.8 fusion.11
  11.4 53.0 %all-gather = bf16[32,20,640]{2,1,0:T(8,128)(2,1)S(1)} all-gather(bf16[1,20,640]{2,1,0:T(8,128)(2,1)S(1)} %fusion.11), channel_id=1, replica_groups=mesh['pair'=32,'red'=8] {'pair'}, dimensions={0}, use_global_device_ids=true | all-gather | bytes 844800 | tf_op jit(solution)/shard_map/all_gather | solution.py:38
  64.6 4.0 %compare_select_fusion = bf16[64,64,640]{2,1,0:T(8,128)(2,1)S(1)} fusion(bf16[64,64,640]{2,1,0:T(8,128)(2,1)} %param.7, s32[64,640]{1,0:T(8,128)S(1)} %broadcast_xor_fusion, s32[64]{0:T(128)} %param.11), kind=kLoop, calls=%fused_computation.2 | loop fusion | flops 5242880 | bytes 10649856 | tf_op jit(solution)/shard_map/jit(_where)/select_n | solution.py:32
  68.6 6.8 %add_convert_fusion = bf16[4096,640]{1,0:T(8,128)(2,1)} fusion(bf16[4096,640]{1,0:T(8,128)(2,1)S(1)} %bitcast.46, bf16[640,640]{1,0:T(8,128)(2,1)S(1)} %reshape.277), kind=kOutput, calls=%fused_computation.1 | convolution fusion | flops 3363307520 | bytes 11304960 | tf_op jit(solution)/shard_map/dot_general | solution.py:39
  75.4 9.4 %reshape.266 = bf16[64,320,128]{2,1,0:T(8,128)(2,1)} reshape(bf16[4096,640]{1,0:T(8,128)(2,1)} %add_convert_fusion) | data formatting | bytes 10485760 | tf_op jit(solution)/shard_map/reshape | solution.py:41
  84.8 8.2 %copy.12 = bf16[64,320,128]{2,0,1:T(8,128)(2,1)} copy(bf16[64,320,128]{2,1,0:T(8,128)(2,1)} %reshape.266) | data formatting | bytes 10485760 | tf_op jit(solution)/shard_map/reshape | solution.py:41
  93.2 6.1 %gather_fusion = bf16[320,64,128]{2,1,0:T(8,128)(2,1)} fusion(bf16[64,320,128]{2,0,1:T(8,128)(2,1)} %copy.12, s32[1024]{0:T(1024)S(1)} %pad_clamp_fusion), kind=kCustom, calls=%fused_computation | custom fusion | bytes 10487040 | tf_op jit(solution)/shard_map/jit(_take)/gather | solution.py:44
  99.3 5.9 %broadcast_select_fusion = bf16[64,32,10,128]{3,0,2,1:T(8,128)(2,1)} fusion(bf16[64,32,10,128]{3,0,2,1:T(8,128)(2,1)} %bitcast.44, pred[32,10]{1,0:T(8,128)(4,1)S(1)} %compare_and_fusion), kind=kLoop, calls=%fused_computation.6 | loop fusion | flops 2621440 | bytes 10486080 | tf_op jit(solution)/shard_map/jit(_take)/select_n | solution.py:44
  105.3 6.8 %all-to-all-start = ((bf16[64,32,10,128]{3,0,2,1:T(8,128)(2,1)}), bf16[64,32,10,128]{3,0,2,1:T(8,128)(2,1)}, u32[]{:S(2)}, u32[]{:S(2)}) async-start(bf16[64,32,10,128]{3,0,2,1:T(8,128)(2,1)} %broadcast_select_fusion), calls=%async_computation | async-start | bytes 10485760 | tf_op jit(solution)/shard_map/all_to_all | solution.py:63
  112.1 0.2 reduce-scatter.2.cloned.1.call-start
  112.3 0.2 fusion.12
  112.5 0.2 divide_reduce_fusion
  112.7 0.8 fusion.17
  114.0 0.3 select_reduce_fusion.1
  114.3 0.6 select_reduce_fusion
  115.1 104.2 %all-to-all-done = bf16[64,32,10,128]{3,0,2,1:T(8,128)(2,1)} async-done(((bf16[64,32,10,128]{3,0,2,1:T(8,128)(2,1)}), bf16[64,32,10,128]{3,0,2,1:T(8,128)(2,1)}, u32[]{:S(2)}, u32[]{:S(2)}) %all-to-all-start) | async-done | bytes 5242912 | tf_op jit(solution)/shard_map/all_to_all | solution.py:63
  219.3 11.8 %copy.13 = bf16[32,64,1,10,128]{4,3,1,0,2:T(8,128)(2,1)S(1)} copy(bf16[32,64,1,10,128]{4,1,3,0,2:T(8,128)(2,1)} %bitcast.6) | data formatting | bytes 10485760 | tf_op jit(solution)/shard_map/all_to_all | solution.py:63
  231.1 4.4 %fusion.3 = bf16[2048,512]{1,0:T(8,128)(2,1)} fusion(bf16[256,8,10,128]{3,2,1,0:T(8,128)(2,1)S(1)} %bitcast.45, bf16[1,1,1280,512]{3,2,1,0:T(8,128)(2,1)S(1)} %copy-done.2, s32[512]{0:T(512)S(1)} %xor_bitcast_fusion.1, s32[1280]{0:T(1024)S(1)} %xor_bitcast_fusion), kind=kOutput, calls=%fused_computation.9 | convolution fusion | flops 2686713856 | bytes 8657920 | tf_op jit(solution)/shard_map/dot_general | solution.py:66
  235.5 33.2 %reduce-scatter.2.cloned.1.call-done = bf16[256,512]{1,0:T(8,128)(2,1)} async-done(((bf16[2048,512]{1,0:T(8,128)(2,1)}), bf16[256,512]{1,0:T(8,128)(2,1)}) %reduce-scatter.2.cloned.1.call-update) | async-done | bytes 262160 | tf_op jit(solution)/shard_map/reduce_scatter | solution.py:65
  (20 shorter events, 1.0 us)
Async XLA Ops:
  105.3 7.0 %copy-start.1 = (s32[32,4]{0,1:T(4,128)S(1)}, s32[32,4]{0,1:T(4,128)}, u32[]{:S(2)}) copy-start(s32[32,4]{0,1:T(4,128)} %param.13) | copy-start | bytes 1540
  105.3 8.2 %copy-start = (s32[640]{0:T(1024)S(1)}, s32[640]{0:T(1024)}, u32[]{:S(2)}) copy-start(s32[640]{0:T(1024)} %param.10) | copy-start | bytes 7684
  105.3 114.0 %all-to-all-start = ((bf16[64,32,10,128]{3,0,2,1:T(8,128)(2,1)}), bf16[64,32,10,128]{3,0,2,1:T(8,128)(2,1)}, u32[]{:S(2)}, u32[]{:S(2)}) async-start(bf16[64,32,10,128]{3,0,2,1:T(8,128)(2,1)} %broadcast_select_fusion), calls=%async_computation | async-start | bytes 10485760 | tf_op jit(solution)/shard_map/all_to_all | solution.py:63
  112.1 156.6 %reduce-scatter.2.cloned.1.call-start = ((), (), s32[]{:S(2)}) async-start(), calls=%async_computation.2 | async-start | bytes 2359296 | tf_op jit(solution)/shard_map/reduce_scatter | solution.py:65
  219.3 11.8 %copy-start.2 = (bf16[1,1,1280,512]{3,2,1,0:T(8,128)(2,1)S(1)}, bf16[1,1,1280,512]{3,2,1,0:T(8,128)(2,1)}, u32[]{:S(2)}) copy-start(bf16[1,1,1280,512]{3,2,1,0:T(8,128)(2,1)} %param.9) | copy-start | bytes 3932164
Sparse Core Ops, SparseCore 0:
  235.6 33.0 reduce-scatter.1
where the time goes:
time: 276 us
  waiting for transfers between devices  137 us (50%)
  blocking collectives  53 us (19%)
  local copies, waits for them, and re-layouts  36.6 us (13%)
  other arithmetic  16.8 us (6%)
  between operations  13.5 us (5%)
  matrix products  11.2 us (4%)
  starting transfers between devices  7.01 us (3%)
    all_to_all x1, waiting for transfers between devices, shards(): lax.all_to_all(ordered, 'pair', split_axis=1, concat_axis=0, tiled=True)  104 us
    all_gather x1, blocking collectives, shards(): gathered_cycle = lax.all_gather(blocked, 'pair', axis=0, tiled=True)  53 us
    reduce_scatter x1, waiting for transfers between devices, shards(): lax.psum_scatter(jnp.dot(owned, masked, preferred_element_type=jnp.float3...  33.2 us
    reshape x2, local copies, waits for them, and re-layouts, shards(): tiles_local = dressed.reshape(local_pairs, slab_rows * block_count, 128)  17.6 us
    all_to_all x1, local copies, waits for them, and re-layouts, shards(): lax.all_to_all(ordered, 'pair', split_axis=1, concat_axis=0, tiled=True)  11.8 us
    dot_general x1, matrix products, shards(): jnp.dot(flattened, gathered_cycle, preferred_element_type=jnp.float32)  6.8 us
    all_to_all x1, starting transfers between devices, shards(): lax.all_to_all(ordered, 'pair', split_axis=1, concat_axis=0, tiled=True)  6.79 us
    select_n x2, other arithmetic, shards(): jnp.take(tiles_local, slot_order, axis=1)  6.67 us
  transfers between devices with their start and end apart: 2, of which 2 were waited for; matrix products, arithmetic and copies ran while one was open for 1% of the time, Pallas kernels for 0%

commit v1 on v0

--- a/solution.py
+++ b/solution.py
@@ -35,7 +35,10 @@
     cycle_keep = irrep_lookup(orbital_irrep, c_local)[:, None] == orbital_irrep[None, :]
     blocked = jnp.where(cycle_keep, cycle_integrals, jnp.zeros_like(cycle_integrals))
     flattened = symmetric.reshape(local_pairs * slab_rows, width_all)
-    gathered_cycle = lax.all_gather(blocked, "pair", axis=0, tiled=True)
+    devices = lax.axis_size("pair")
+    pieces = jnp.stack([blocked for _ in range(devices)])
+    pieces = lax.all_to_all(pieces, "pair", split_axis=0, concat_axis=0)
+    gathered_cycle = jnp.concatenate(pieces, axis=0)
     cycle = jnp.dot(flattened, gathered_cycle, preferred_element_type=jnp.float32)
     dressed = (flattened.astype(jnp.float32) + cycle).astype(jnp.bfloat16)
     tiles_local = dressed.reshape(local_pairs, slab_rows * block_count, 128)

time: 276 us -> 267 us (0.967)
  blocking collectives: 53 us -> 0 us
  waiting for transfers between devices: 137 us -> 164 us
  starting transfers between devices: 7.01 us -> 17.7 us
  matrix products: 11.2 us -> 14.8 us
    all_gather x1 -> x0, blocking collectives: 53 us -> none  [shards(): gathered_cycle = lax.all_gather(blocked, 'pair', axis=0, tiled=True)]
    all_to_all x0 -> x1, waiting for transfers between devices: none -> 17 us  [shards(): pieces = lax.all_to_all(pieces, 'pair', split_axis=0, concat_axis=0)]
    all_to_all x0 -> x1, starting transfers between devices: none -> 11.7 us  [shards(): pieces = lax.all_to_all(pieces, 'pair', split_axis=0, concat_axis=0)]
    all_to_all x1, waiting for transfers between devices: 104 us -> 115 us  [shards(): lax.all_to_all(ordered, 'pair', split_axis=1, concat_axis=0, tiled=True)]
    dot_general x1, matrix products: 6.8 us -> 10.5 us  [shards(): jnp.dot(flattened, gathered_cycle, preferred_element_type=jnp.float32)]
  transfers between devices with their start and end apart: 2 -> 3, of which waited for: 2 -> 3; matrix products, arithmetic and copies ran while one was open for 1% -> 5% of each run, Pallas kernels for 0% -> 0%
where the time goes in v1:
time: 267 us
  waiting for transfers between devices  164 us (61%)
  local copies, waits for them, and re-layouts  37.6 us (14%)
  other arithmetic  19.2 us (7%)
  starting transfers between devices  17.7 us (7%)
  matrix products  14.8 us (6%)
  between operations  13.5 us (5%)
    all_to_all x1, waiting for transfers between devices, shards(): lax.all_to_all(ordered, 'pair', split_axis=1, concat_axis=0, tiled=True)  115 us
    reduce_scatter x1, waiting for transfers between devices, shards(): lax.psum_scatter(jnp.dot(owned, masked, preferred_element_type=jnp.float3...  32.1 us
    reshape x2, local copies, waits for them, and re-layouts, shards(): tiles_local = dressed.reshape(local_pairs, slab_rows * block_count, 128)  17.6 us
    all_to_all x1, waiting for transfers between devices, shards(): pieces = lax.all_to_all(pieces, 'pair', split_axis=0, concat_axis=0)  17 us
    all_to_all x1, local copies, waits for them, and re-layouts, shards(): lax.all_to_all(ordered, 'pair', split_axis=1, concat_axis=0, tiled=True)  11.8 us
    all_to_all x1, starting transfers between devices, shards(): pieces = lax.all_to_all(pieces, 'pair', split_axis=0, concat_axis=0)  11.7 us
    dot_general x1, matrix products, shards(): jnp.dot(flattened, gathered_cycle, preferred_element_type=jnp.float32)  10.5 us
    select_n x2, other arithmetic, shards(): jnp.take(tiles_local, slot_order, axis=1)  6.68 us
  transfers between devices with their start and end apart: 3, of which 3 were waited for; matrix products, arithmetic and copies ran while one was open for 5% of the time, Pallas kernels for 0%

profile of v1, /device:TPU:8, one launch (start us, length us, event | category | flops | bytes accessed | tf_op | source)
XLA Modules:
  0.0 266.6 jit_solution(9870551647190035924)
XLA Ops:
  6.5 0.9 select_reduce_fusion.3
  7.4 0.8 compare_select_fusion.2
  8.3 1.1 stack.2
  9.3 11.7 %all-to-all-start = ((bf16[32,20,640]{2,1,0:T(8,128)(2,1)}), bf16[32,20,640]{2,1,0:T(8,128)(2,1)S(1)}, u32[]{:S(2)}, u32[]{:S(2)}) async-start(bf16[32,20,640]{2,1,0:T(8,128)(2,1)} %stack.2), calls=%async_computation | async-start | bytes 1966080 | tf_op jit(solution)/shard_map/all_to_all | solution.py:40
  21.0 0.7 dynamic-slice_reduce_fusion
  21.9 0.7 fusion.13
  22.6 0.9 select_reduce_fusion.2
  23.5 0.8 broadcast_xor_fusion
  24.3 6.4 %compare_select_fusion = bf16[64,64,640]{2,1,0:T(8,128)(2,1)} fusion(bf16[64,64,640]{2,1,0:T(8,128)(2,1)} %param.7, s32[64,640]{1,0:T(8,128)S(1)} %broadcast_xor_fusion, s32[64]{0:T(128)} %param.11), kind=kLoop, calls=%fused_computation.2 | loop fusion | flops 5242880 | bytes 10649856 | tf_op jit(solution)/shard_map/jit(_where)/select_n | solution.py:32
  30.7 17.0 %all-to-all-done = bf16[32,20,640]{2,1,0:T(8,128)(2,1)S(1)} async-done(((bf16[32,20,640]{2,1,0:T(8,128)(2,1)}), bf16[32,20,640]{2,1,0:T(8,128)(2,1)S(1)}, u32[]{:S(2)}, u32[]{:S(2)}) %all-to-all-start) | async-done | bytes 819232 | tf_op jit(solution)/shard_map/all_to_all | solution.py:40
  47.8 10.5 %add_convert_fusion = bf16[4096,640]{1,0:T(8,128)(2,1)} fusion(bf16[4096,640]{1,0:T(8,128)(2,1)} %bitcast.44, bf16[640,640]{1,0:T(8,128)(2,1)S(1)} %reshape.271), kind=kOutput, calls=%fused_computation.1 | convolution fusion | flops 3363307520 | bytes 11304960 | tf_op jit(solution)/shard_map/dot_general | solution.py:42
  58.3 9.4 %reshape.272 = bf16[64,320,128]{2,1,0:T(8,128)(2,1)} reshape(bf16[4096,640]{1,0:T(8,128)(2,1)} %add_convert_fusion) | data formatting | bytes 10485760 | tf_op jit(solution)/shard_map/reshape | solution.py:44
  67.7 8.2 %copy.10 = bf16[64,320,128]{2,0,1:T(8,128)(2,1)} copy(bf16[64,320,128]{2,1,0:T(8,128)(2,1)} %reshape.272) | data formatting | bytes 10485760 | tf_op jit(solution)/shard_map/reshape | solution.py:44
  75.9 6.1 %gather_fusion = bf16[320,64,128]{2,1,0:T(8,128)(2,1)} fusion(bf16[64,320,128]{2,0,1:T(8,128)(2,1)} %copy.10, s32[1024]{0:T(1024)S(1)} %pad_clamp_fusion), kind=kCustom, calls=%fused_computation | custom fusion | bytes 10487040 | tf_op jit(solution)/shard_map/jit(_take)/gather | solution.py:47
  82.1 5.9 %broadcast_select_fusion = bf16[64,32,10,128]{3,0,2,1:T(8,128)(2,1)} fusion(bf16[64,32,10,128]{3,0,2,1:T(8,128)(2,1)} %bitcast.42, pred[32,10]{1,0:T(8,128)(4,1)S(1)} %compare_and_fusion), kind=kLoop, calls=%fused_computation.6 | loop fusion | flops 2621440 | bytes 10486080 | tf_op jit(solution)/shard_map/jit(_take)/select_n | solution.py:47
  88.0 5.7 %all-to-all-start.1 = ((bf16[64,32,10,128]{3,0,2,1:T(8,128)(2,1)}), bf16[64,32,10,128]{3,0,2,1:T(8,128)(2,1)}, u32[]{:S(2)}, u32[]{:S(2)}) async-start(bf16[64,32,10,128]{3,0,2,1:T(8,128)(2,1)} %broadcast_select_fusion), calls=%async_computation.1 | async-start | bytes 10485760 | tf_op jit(solution)/shard_map/all_to_all | solution.py:66
  93.8 0.2 reduce-scatter.2.cloned.1.call-start
  94.4 0.8 fusion.16
  95.7 0.3 select_reduce_fusion.1
  96.0 0.6 select_reduce_fusion
  96.8 114.6 %all-to-all-done.1 = bf16[64,32,10,128]{3,0,2,1:T(8,128)(2,1)} async-done(((bf16[64,32,10,128]{3,0,2,1:T(8,128)(2,1)}), bf16[64,32,10,128]{3,0,2,1:T(8,128)(2,1)}, u32[]{:S(2)}, u32[]{:S(2)}) %all-to-all-start.1) | async-done | bytes 5242912 | tf_op jit(solution)/shard_map/all_to_all | solution.py:66
  211.4 11.8 %copy.11 = bf16[32,64,1,10,128]{4,3,1,0,2:T(8,128)(2,1)S(1)} copy(bf16[32,64,1,10,128]{4,1,3,0,2:T(8,128)(2,1)} %bitcast.5) | data formatting | bytes 10485760 | tf_op jit(solution)/shard_map/all_to_all | solution.py:66
  223.2 4.4 %fusion.3 = bf16[2048,512]{1,0:T(8,128)(2,1)} fusion(bf16[256,8,10,128]{3,2,1,0:T(8,128)(2,1)S(1)} %bitcast.43, bf16[1,1,1280,512]{3,2,1,0:T(8,128)(2,1)S(1)} %copy-done.2, s32[512]{0:T(512)S(1)} %xor_bitcast_fusion.1, s32[1280]{0:T(1024)S(1)} %xor_bitcast_fusion), kind=kOutput, calls=%fused_computation.9 | convolution fusion | flops 2686713856 | bytes 8657920 | tf_op jit(solution)/shard_map/dot_general | solution.py:69
  227.6 32.1 %reduce-scatter.2.cloned.1.call-done = bf16[256,512]{1,0:T(8,128)(2,1)} async-done(((bf16[2048,512]{1,0:T(8,128)(2,1)}), bf16[256,512]{1,0:T(8,128)(2,1)}) %reduce-scatter.2.cloned.1.call-update) | async-done | bytes 262160 | tf_op jit(solution)/shard_map/reduce_scatter | solution.py:68
  (22 shorter events, 1.4 us)
Async XLA Ops:
  9.3 38.4 %all-to-all-start = ((bf16[32,20,640]{2,1,0:T(8,128)(2,1)}), bf16[32,20,640]{2,1,0:T(8,128)(2,1)S(1)}, u32[]{:S(2)}, u32[]{:S(2)}) async-start(bf16[32,20,640]{2,1,0:T(8,128)(2,1)} %stack.2), calls=%async_computation | async-start | bytes 1966080 | tf_op jit(solution)/shard_map/all_to_all | solution.py:40
  88.0 6.0 %copy-start.1 = (s32[32,4]{0,1:T(4,128)S(1)}, s32[32,4]{0,1:T(4,128)}, u32[]{:S(2)}) copy-start(s32[32,4]{0,1:T(4,128)} %param.13) | copy-start | bytes 1540
  88.0 7.2 %copy-start = (s32[640]{0:T(1024)S(1)}, s32[640]{0:T(1024)}, u32[]{:S(2)}) copy-start(s32[640]{0:T(1024)} %param.10) | copy-start | bytes 7684
  88.0 123.4 %all-to-all-start.1 = ((bf16[64,32,10,128]{3,0,2,1:T(8,128)(2,1)}), bf16[64,32,10,128]{3,0,2,1:T(8,128)(2,1)}, u32[]{:S(2)}, u32[]{:S(2)}) async-start(bf16[64,32,10,128]{3,0,2,1:T(8,128)(2,1)} %broadcast_select_fusion), calls=%async_computation.1 | async-start | bytes 10485760 | tf_op jit(solution)/shard_map/all_to_all | solution.py:66
  93.8 166.0 %reduce-scatter.2.cloned.1.call-start = ((), (), s32[]{:S(2)}) async-start(), calls=%async_computation.3 | async-start | bytes 2359296 | tf_op jit(solution)/shard_map/reduce_scatter | solution.py:68
  211.4 11.8 %copy-start.2 = (bf16[1,1,1280,512]{3,2,1,0:T(8,128)(2,1)S(1)}, bf16[1,1,1280,512]{3,2,1,0:T(8,128)(2,1)}, u32[]{:S(2)}) copy-start(bf16[1,1,1280,512]{3,2,1,0:T(8,128)(2,1)} %param.9) | copy-start | bytes 3932164
Sparse Core Ops, SparseCore 0:
  227.7 31.9 reduce-scatter.1
